TPU v7x, 32 devices: a whole 2x2x4 slice. The times are simulated.
32 devices in a mesh: dom: 8 (over y, x, core), sub: 4 (over z).
Axes of the slice: x: 2, y: 2, z: 4, core: 2. Of those that a mesh axis runs over, the one named last changes fastest.
Arguments:
- upstream: bfloat16 [65536, 128], P(('dom', 'sub')), may hold values from -6 to 6
- features: bfloat16 [65536, 128], P(('dom', 'sub')), may hold values from -6 to 6
- w_in: bfloat16 [128, 128], replicated, may hold values from -0.5 to 0.5
- w_out: bfloat16 [128, 128], replicated, may hold values from -0.5 to 0.5
- inner_adj: bfloat16 [65536, 2048], P(('dom', 'sub')), may hold values from -0.125 to 0.125
- cut_tiles: bfloat16 [768, 128, 128], P(('dom', 'sub')), may hold values from -0.15625 to 0.15625
- cut_list: int32 [768, 3], P(('dom', 'sub')), may hold values from 0 to 511, as said below
- cut_count: int32 [32], P(('dom', 'sub')), may hold values from 1 to 24, as said below
Outputs:
- input_grad: bfloat16 [65536, 128], P(('dom', 'sub'))
- grad_w_in: float32 [128, 128], replicated
- grad_w_out: float32 [128, 128], replicated
Inputs may be any that keep to these rules, and one draw needn't show every extreme that they name: `cut_list`: device s's list has 24 rows; column 0 is a local block below 16, column 1 a global block whose device is not s, column 2 a tile id below 24, all tile ids of one device distinct. Among the first cut_count[s] rows the devices of column 1 are all distinct, so one device sends at most one block to another. `cut_count`: some device has exactly 24 live entries in every draw.
All inputs are finite; a program needn't handle non-finite values.
Results may differ from a plain program's by a relative error of at most 0.015.
Values may be sent and summed in bfloat16 or wider, within the bound.
A program may use at most 128 MiB of HBM per device.

v0:
```python
import functools
import math

import jax
import jax.numpy as jnp
from jax import lax
from jax.experimental import pallas as pl
from jax.experimental.pallas import tpu as pltpu
from jax.sharding import PartitionSpec as P

STEPS = 4
teleport = 0.1
MESH = pl.DeviceIdType.MESH
F32 = jnp.float32
BF16 = jnp.bfloat16


def nt_dot(a, b):
    return lax.dot_general(a, b, (((1,), (1,)), ((), ())), preferred_element_type=F32)


def tn_dot(a, b):
    return lax.dot_general(a, b, (((0,), (0,)), ((), ())), preferred_element_type=F32)


def kernel(
    n_dom, n_sub, norm_scale,
    idx_ref, up_ref, tiles_ref, ids_out, w_in_ref, w_out_ref, adj_hbm, feat_hbm,
    dpre, gfull,
    adj, feat, v, outb, arrived, ids_in, acc, accum, fac, act, gsend, gparts, gred,
    local_sem, send_sem, recv_sem, id_send, id_recv,
):
    n = n_dom * n_sub
    my_dom, my_sub = lax.axis_index("dom"), lax.axis_index("sub")
    me = my_dom * n_sub + my_sub
    nb, blk, width = up_ref.shape
    rows = nb * blk
    tile = min(512, rows)
    blocks = tile // blk
    paired = n_sub & (n_sub - 1) == 0
    pairings = list(reversed(range(n_sub)))
    arrivals = [(0, 1, n_dom)]
    for m in pairings[:-1]:
        arrivals += [(m, i, min(i + 2, n_dom)) for i in range(0, n_dom, 2)] if m == 1 else [(m, 0, n_dom // 2), (m, n_dom // 2, n_dom)]

    def partner(m, sign):
        if not paired:
            return lax.rem(my_sub + sign * m + n_sub, n_sub)
        z, bit = my_sub, 1
        while bit < n_sub:
            if m & bit:
                z = z + bit - 2 * bit * lax.rem(my_sub // bit, 2)
            bit *= 2
        return z

    def peer(m, i, sign=1):
        d = lax.rem(my_dom + sign * i + n_dom, n_dom)
        z = partner(m, sign)
        return d, z, d * n_sub + z

    def each_peer(fn):
        for m in pairings:
            def body(i, carry, m=m):
                fn(*peer(m, i))
                return carry
            lax.fori_loop(1 if m == 0 else 0, n_dom, body, 0, unroll=m != 0)

    adj_copy = pltpu.make_async_copy(adj_hbm, adj, local_sem.at[0])
    feat_copy = pltpu.make_async_copy(feat_hbm, feat, local_sem.at[1])
    adj_copy.start()
    feat_copy.start()

    barrier = pltpu.get_barrier_semaphore()
    each_peer(lambda d, z, t: pl.semaphore_signal(
        barrier, inc=1, device_id=(d, z), device_id_type=MESH))
    pl.semaphore_wait(barrier, n - 1)

    def id_copy(d, z, t, slot):
        return pltpu.make_async_remote_copy(
            src_ref=ids_out.at[t], dst_ref=ids_in.at[slot], send_sem=id_send.at[t],
            recv_sem=id_recv.at[slot], device_id=(d, z), device_id_type=MESH)

    def block_copy(p, d, z, t, slot):
        return pltpu.make_async_remote_copy(
            src_ref=outb.at[p, t], dst_ref=arrived.at[p, slot], send_sem=send_sem.at[p, t],
            recv_sem=recv_sem.at[p, slot], device_id=(d, z), device_id_type=MESH)

    each_peer(lambda d, z, t: id_copy(d, z, t, me).start())
    v[...] = up_ref[...]
    accum[...] = jnp.zeros_like(accum)

    for step in range(STEPS):
        p = step % 2

        def send(d, z, t):
            if step >= 2:
                block_copy(p, d, z, t, t).wait_send()
            product = jnp.dot(tiles_ref[idx_ref[2, t]], v[idx_ref[0, t]], preferred_element_type=F32)
            outb[p, t] = product.astype(BF16)
            block_copy(p, d, z, t, me).start()

        each_peer(send)

        if step == 0:
            feat_copy.wait()

            def head(i, carry):
                at = pl.ds(pl.multiple_of(i * tile, tile), tile)
                pre = jnp.dot(feat[at, :], w_in_ref[...], preferred_element_type=F32)
                gate = jax.nn.sigmoid(pre)
                act[at, :] = (pre * gate).astype(BF16)
                fac[at, :] = gate * (1.0 + pre * (1.0 - gate))
                return carry

            lax.fori_loop(0, rows // tile, head, 0)
            adj_copy.wait()

        def local(i, carry):
            at = pl.ds(pl.multiple_of(i * tile, tile), tile)
            term = jnp.dot(adj[at, :], v[...].reshape(rows, width), preferred_element_type=F32)
            ats = pl.ds(i * blocks, blocks)
            acc[ats] = term.reshape(blocks, blk, width)
            accum[ats] += teleport * v[ats].astype(F32)
            return carry

        lax.fori_loop(0, rows // tile, local, 0)

        for m, first, end in arrivals:
            last = (m, first, end) == arrivals[-1]

            def arrive(i, carry):
                d, z, s = peer(m, i, -1)
                if step == 0:
                    id_copy(d, z, s, s).wait_recv()
                block_copy(p, d, z, s, s).wait_recv()
                return carry

            lax.fori_loop(first, end, arrive, 0)

            def gather(b, carry):
                total = acc[b]
                for i in range(first, end):
                    s = peer(m, i, -1)[2]
                    hit = ids_in[s, 0:1, :] == b
                    total += jnp.where(hit, arrived[p, s].astype(F32), 0.0)
                if last:
                    v[b] = ((1.0 - teleport) * total).astype(BF16)
                else:
                    acc[b] = total
                return carry

            lax.fori_loop(0, nb, gather, 0, unroll=4)

    def wait_sends(d, z, t):
        id_copy(d, z, t, t).wait_send()
        block_copy(0, d, z, t, t).wait_send()
        block_copy(1, d, z, t, t).wait_send()

    hid = w_in_ref.shape[1]
    feats = w_in_ref.shape[0]

    def tail(i, carry):
        part_in, part_out = carry
        at = pl.ds(pl.multiple_of(i * tile, tile), tile)
        ats = pl.ds(i * blocks, blocks)
        grad = (accum[ats] + v[ats].astype(F32)).astype(BF16).reshape(tile, width)
        part_out += tn_dot(act[at, :], grad)
        back = nt_dot(grad, w_out_ref[...])
        inner = (back * fac[at, :]).astype(BF16)
        dpre[at, :] = inner
        part_in += tn_dot(feat[at, :], inner)
        return part_in, part_out

    part_in, part_out = lax.fori_loop(
        0, rows // tile, tail,
        (jnp.zeros((feats, hid), F32), jnp.zeros((hid, width), F32)))
    chunk = gred.shape[0]
    owners = gsend.shape[0]
    gsend[0:feats // chunk] = (part_in * norm_scale).reshape(feats // chunk, chunk, hid).astype(BF16)
    gsend[feats // chunk:owners] = (part_out * norm_scale).reshape(hid // chunk, chunk, width).astype(BF16)
    each_peer(wait_sends)

    def part_copy(d, z, t, slot):
        return pltpu.make_async_remote_copy(
            src_ref=gsend.at[t], dst_ref=gparts.at[slot], send_sem=send_sem.at[0, t],
            recv_sem=recv_sem.at[0, slot], device_id=(d, z), device_id_type=MESH)

    def sum_copy(d, z, t, own, slot):
        return pltpu.make_async_remote_copy(
            src_ref=gred, dst_ref=gfull.at[own], send_sem=send_sem.at[1, t],
            recv_sem=recv_sem.at[1, slot], device_id=(d, z), device_id_type=MESH)

    def when_owner(t, fn):
        if owners == n:
            fn()
        else:
            pl.when(t < owners)(fn)

    each_peer(lambda d, z, t: when_owner(t, lambda: part_copy(d, z, t, me).start()))

    def reduce():
        each_peer(lambda d, z, s: pltpu.make_async_remote_copy(
            src_ref=gsend.at[0], dst_ref=gparts.at[s], send_sem=send_sem.at[0, s],
            recv_sem=recv_sem.at[0, s], device_id=(d, z), device_id_type=MESH).wait_recv())
        gparts[me] = gsend[me]

        def add(i, total):
            return total + gparts[i].astype(F32)

        total = lax.fori_loop(1, n, add, gparts[0].astype(F32)).astype(BF16)
        gred[...] = total
        gfull[me] = total
        each_peer(lambda d, z, t: sum_copy(d, z, t, me, me).start())

    when_owner(me, reduce)
    each_peer(lambda d, z, t: when_owner(t, lambda: part_copy(d, z, t, t).wait_send()))
    each_peer(lambda d, z, s: when_owner(s, lambda: sum_copy(d, z, s, s, s).wait_recv()))
    when_owner(me, lambda: each_peer(lambda d, z, t: sum_copy(d, z, t, me, me).wait_send()))


def finish(dpre_ref, w_in_ref, gfull_ref, ig_ref, gin_ref, gout_ref):
    owners, chunk, _ = gfull_ref.shape
    split = gin_ref.shape[0] // chunk
    ig_ref[...] = nt_dot(dpre_ref[...], w_in_ref[...]).astype(BF16)
    gin_ref[...] = gfull_ref[0:split].astype(F32).reshape(gin_ref.shape)
    gout_ref[...] = gfull_ref[split:owners].astype(F32).reshape(gout_ref.shape)


def on_device(n_dom, n_sub, upstream, features, w_in, w_out, inner_adj, cut_tiles, cut_list, cut_count):
    n = n_dom * n_sub
    rows, width = upstream.shape
    entries, blk, _ = cut_tiles.shape
    nb = rows // blk
    feats, hid = w_in.shape
    live = jnp.arange(entries, dtype=jnp.int32) < cut_count[0]
    owner = jnp.where(live, cut_list[:, 1] // nb, n)
    picked = owner[None, :] == jnp.arange(n, dtype=jnp.int32)[:, None]
    idx = jnp.sum(jnp.where(picked[None], cut_list.T[:, None, :], 0), axis=2)
    block_id = jnp.where(jnp.any(picked, axis=1), idx[1] % nb, nb)
    ids = jnp.broadcast_to(block_id[:, None, None], (n, 1, 128))
    grad_rows = feats + hid
    chunk = max(8, grad_rows // n)
    owners = grad_rows // chunk
    vmem = pl.BlockSpec(memory_space=pltpu.VMEM)
    hbm = pl.BlockSpec(memory_space=pl.ANY)
    scratch = [
        pltpu.VMEM(inner_adj.shape, BF16),
        pltpu.VMEM(features.shape, BF16),
        pltpu.VMEM((nb, blk, width), BF16),
        pltpu.VMEM((2, n, blk, width), BF16),
        pltpu.VMEM((2, n, blk, width), BF16),
        pltpu.VMEM((n, 1, 128), jnp.int32),
        pltpu.VMEM((nb, blk, width), F32),
        pltpu.VMEM((nb, blk, width), F32),
        pltpu.VMEM((rows, hid), F32),
        pltpu.VMEM((rows, hid), BF16),
        pltpu.VMEM((owners, chunk, hid), BF16),
        pltpu.VMEM((n, chunk, hid), BF16),
        pltpu.VMEM((chunk, hid), BF16),
        pltpu.SemaphoreType.DMA((2,)),
        pltpu.SemaphoreType.DMA((2, n)),
        pltpu.SemaphoreType.DMA((2, n)),
        pltpu.SemaphoreType.DMA((n,)),
        pltpu.SemaphoreType.DMA((n,)),
    ]
    dpre, sums = pl.pallas_call(
        functools.partial(kernel, n_dom, n_sub, 1.0 / math.sqrt(rows * n)),
        out_shape=(
            jax.ShapeDtypeStruct((rows, hid), BF16),
            jax.ShapeDtypeStruct((owners, chunk, hid), BF16),
        ),
        in_specs=[pl.BlockSpec(memory_space=pltpu.SMEM)] + [vmem] * 5 + [hbm] * 2,
        out_specs=(vmem, vmem),
        scratch_shapes=scratch,
        compiler_params=pltpu.CompilerParams(collective_id=0, has_side_effects=True),
    )(idx, upstream.reshape(nb, blk, width), cut_tiles, ids, w_in, w_out, inner_adj, features)
    return pl.pallas_call(
        finish,
        out_shape=(
            jax.ShapeDtypeStruct((rows, feats), BF16),
            jax.ShapeDtypeStruct((feats, hid), F32),
            jax.ShapeDtypeStruct((hid, width), F32),
        ),
        in_specs=[vmem] * 3,
        out_specs=(vmem, vmem, vmem),
    )(dpre, w_in, sums)


def solution(mesh):
    both = ("dom", "sub")
    placed = (
        P(both, None),
        P(both, None),
        P(),
        P(),
        P(both, None),
        P(both, None, None),
        P(both, None),
        P(both),
    )
    return jax.shard_map(
        functools.partial(on_device, mesh.shape["dom"], mesh.shape["sub"]),
        mesh=mesh,
        in_specs=placed,
        out_specs=(P(both, None), P(), P()),
        check_vma=False,
    )
```

profile of v0, /device:TPU:0, one launch (start us, length us, event | category | flops | bytes accessed | tf_op | source)
XLA Modules:
  0.0 124.0 jit_solution(382772807705742034)
XLA Ops:
  1.3 0.7 compare_select_fusion.2
  2.0 0.1 fusion.2
  2.1 0.8 select_reduce_fusion.idx_ref
  2.8 0.0 copy-start
  2.9 0.7 broadcast_in_dim.40.ids_out
  3.6 0.0 copy-done
  3.6 118.3 %shard_map.103 = (bf16[2048,128]{1,0:T(8,128)(2,1)}, bf16[32,8,128]{2,1,0:T(8,128)(2,1)}) custom-call(s32[3,32]{1,0:T(4,128)} %copy-done, bf16[16,128,128]{2,1,0:T(8,128)(2,1)} %bitcast.16, bf16[24,128,128]{2,1,0:T(8,128)(2,1)} %tiles_ref.1, s32[32,1,128]{2,1,0:T(1,128)} %broadcast_in_dim.40.ids_out, bf16[128,128]{1,0:T(8,128)(2,1)} %w_in_ref.3, ...), custom_call_target="tpu_custom_call" | custom-call | tf_op jit(solution)/shard_map/pallas_call | solution.py:266
  121.8 2.2 %shard_map.104 = (bf16[2048,128]{1,0:T(8,128)(2,1)}, f32[128,128]{1,0:T(8,128)}, f32[128,128]{1,0:T(8,128)}) custom-call(bf16[2048,128]{1,0:T(8,128)(2,1)} %get-tuple-element.5.dpre_ref, bf16[128,128]{1,0:T(8,128)(2,1)} %w_in_ref.3, bf16[32,8,128]{2,1,0:T(8,128)(2,1)} %get-tuple-element.6.gfull_ref), custom_call_target="tpu_custom_call" | custom-call | tf_op jit(solution)/shard_map/pallas_call | solution.py:277
  (1 shorter events, 0.0 us)
Async XLA Ops:
  2.8 0.7 copy-start
where the time goes:
time: 124 us
  Pallas kernels  120 us (97%)
  other arithmetic  1.57 us (1%)
  between operations  1.3 us (1%)
    pallas_call x1, Pallas kernels, on_device(): pl.pallas_call(functools.partial(kernel, n_dom, n_sub, 1.0 / math.sqrt(ro...  118 us

commit v1 on v0

v1 whole, which is shorter than its diff:
```python
import functools
import math

import jax
import jax.numpy as jnp
from jax import lax
from jax.experimental import pallas as pl
from jax.experimental.pallas import tpu as pltpu
from jax.sharding import PartitionSpec as P

STEPS = 4
teleport = 0.1
MESH = pl.DeviceIdType.MESH
F32 = jnp.float32
BF16 = jnp.bfloat16
I32 = jnp.int32


def nt_dot(a, b):
    return lax.dot_general(a, b, (((1,), (1,)), ((), ())), preferred_element_type=F32)


def nn_dot(a, b):
    return jnp.dot(a, b, preferred_element_type=F32)


def owner_layout(n_dom, n_sub, grad_rows):
    low = n_sub // 4
    width = n_sub - 2 * low
    chunk = max(8, grad_rows // (n_dom * width))
    return low, width, grad_rows // chunk, chunk


def kernel(
    n_dom, n_sub, norm_scale,
    list_hbm, count_hbm, up_hbm, tiles_hbm, w_in_hbm, w_out_hbm, adj_hbm, feat_hbm,
    dpre_hbm, gfull,
    list_v, count_s, idx_v, idx_s, tiles, w_in, w_out,
    adj, feat, v, outb, arrived, ids_out, ids_in, acc, accum, fac, act_t, feat_t, dpre,
    gsend, gparts, gred,
    local_sem, send_sem, recv_sem, id_send, id_recv, part_send, part_recv, sum_send, sum_recv,
):
    n = n_dom * n_sub
    my_dom, my_sub = lax.axis_index("dom"), lax.axis_index("sub")
    me = my_dom * n_sub + my_sub
    nb, blk, width = v.shape
    rows = nb * blk
    feats, hid = w_in.shape
    tile = min(512, rows)
    blocks = tile // blk
    paired = n_sub & (n_sub - 1) == 0
    pairings = list(reversed(range(n_sub)))
    early = pairings[: n_sub // 2] if n_sub > 1 else []
    arrivals = [(0, 1, n_dom)]
    for m in pairings[:-1]:
        arrivals += [(m, i, min(i + 2, n_dom)) for i in range(0, n_dom, 2)] if m == 1 else [(m, 0, n_dom // 2), (m, n_dom // 2, n_dom)]

    def partner(m, sign):
        if not paired:
            return lax.rem(my_sub + sign * m + n_sub, n_sub)
        z, bit = my_sub, 1
        while bit < n_sub:
            if m & bit:
                z = z + bit - 2 * bit * lax.rem(my_sub // bit, 2)
            bit *= 2
        return z

    def peer(m, i, sign=1):
        d = lax.rem(my_dom + sign * i + n_dom, n_dom)
        z = partner(m, sign)
        return d, z, d * n_sub + z

    def each_peer(fn, chosen=None):
        for m in pairings if chosen is None else chosen:
            def body(i, carry, m=m):
                fn(*peer(m, i))
                return carry
            lax.fori_loop(1 if m == 0 else 0, n_dom, body, 0, unroll=m != 0)

    barrier = pltpu.get_barrier_semaphore()
    each_peer(lambda d, z, t: pl.semaphore_signal(
        barrier, inc=1, device_id=(d, z), device_id_type=MESH))

    loads = [
        pltpu.make_async_copy(src, dst, local_sem.at[i])
        for i, (src, dst) in enumerate([
            (list_hbm, list_v), (count_hbm, count_s), (up_hbm, v), (tiles_hbm, tiles),
            (w_in_hbm, w_in), (w_out_hbm, w_out), (feat_hbm, feat), (adj_hbm, adj)])
    ]
    for load in loads:
        load.start()
    list_load, count_load, up_load, tiles_load, w_in_load, w_out_load, feat_load, adj_load = loads
    list_load.wait()
    count_load.wait()

    entries = list_v.shape[1]
    lanes = idx_v.shape[1]
    first = lax.broadcasted_iota(I32, (n, entries), 0) * nb
    goal = jnp.broadcast_to(list_v[1:2, :], (n, entries))
    live = lax.broadcasted_iota(I32, (n, entries), 1) < count_s[0]
    hit = live & (goal >= first) & (goal < first + nb)

    def pick(values):
        return jnp.sum(jnp.where(hit, values, 0), axis=1, keepdims=True)

    on_diagonal = lax.broadcasted_iota(I32, (n, lanes), 0) == lax.broadcasted_iota(I32, (n, lanes), 1)

    def as_row(column):
        return jnp.sum(jnp.where(on_diagonal, column, 0), axis=0, keepdims=True)

    idx_v[0:1, :] = as_row(pick(list_v[0:1, :]))
    idx_v[1:2, :] = as_row(pick(list_v[2:3, :]))
    idx_copy = pltpu.make_async_copy(idx_v, idx_s, local_sem.at[0])
    idx_copy.start()
    block_id = pick(goal - first - nb) + nb
    ids_out[...] = jnp.broadcast_to(block_id, (n, 128)).reshape(n, 1, 128)
    accum[...] = jnp.zeros_like(accum)

    def id_copy(d, z, t, slot):
        return pltpu.make_async_remote_copy(
            src_ref=ids_out.at[t], dst_ref=ids_in.at[slot], send_sem=id_send.at[t],
            recv_sem=id_recv.at[slot], device_id=(d, z), device_id_type=MESH)

    def block_copy(p, d, z, t, slot):
        return pltpu.make_async_remote_copy(
            src_ref=outb.at[p, t], dst_ref=arrived.at[p, slot], send_sem=send_sem.at[p, t],
            recv_sem=recv_sem.at[p, slot], device_id=(d, z), device_id_type=MESH)

    def multiply(p, t):
        outb[p, t] = nn_dot(tiles[idx_s[1, t]], v[idx_s[0, t]]).astype(BF16)

    idx_copy.wait()
    up_load.wait()
    tiles_load.wait()
    each_peer(lambda d, z, t: multiply(0, t), early)
    pl.semaphore_wait(barrier, n - 1)

    def send_early(d, z, t):
        id_copy(d, z, t, me).start()
        block_copy(0, d, z, t, me).start()

    each_peer(send_early, early)
    late = [m for m in pairings if m not in early]

    for step in range(STEPS):
        p = step % 2

        def send(d, z, t):
            if step >= 2:
                block_copy(p, d, z, t, t).wait_send()
            if step == 0:
                id_copy(d, z, t, me).start()
            multiply(p, t)
            block_copy(p, d, z, t, me).start()

        each_peer(send, late if step == 0 else pairings)

        if step == 0:
            feat_load.wait()
            w_in_load.wait()
            w_out_load.wait()

            def head(i, carry):
                at = pl.ds(pl.multiple_of(i * tile, tile), tile)
                here = feat[at, :]
                pre = nn_dot(here, w_in[...])
                gate = jax.nn.sigmoid(pre)
                act_t[:, at] = (pre * gate).astype(BF16).T
                feat_t[:, at] = here.T
                fac[at, :] = gate * (1.0 + pre * (1.0 - gate))
                return carry

            lax.fori_loop(0, rows // tile, head, 0)
            adj_load.wait()

        def local(i, carry):
            at = pl.ds(pl.multiple_of(i * tile, tile), tile)
            term = nn_dot(adj[at, :], v[...].reshape(rows, width))
            ats = pl.ds(i * blocks, blocks)
            acc[ats] = term.reshape(blocks, blk, width)
            accum[ats] += teleport * v[ats].astype(F32)
            return carry

        lax.fori_loop(0, rows // tile, local, 0)

        for m, start, end in arrivals:
            last = (m, start, end) == arrivals[-1]

            def arrive(i, carry):
                d, z, s = peer(m, i, -1)
                if step == 0:
                    id_copy(d, z, s, s).wait_recv()
                block_copy(p, d, z, s, s).wait_recv()
                return carry

            lax.fori_loop(start, end, arrive, 0)

            def gather(b, carry):
                total = acc[b]
                for i in range(start, end):
                    s = peer(m, i, -1)[2]
                    match = ids_in[s, 0:1, :] == b
                    total += jnp.where(match, arrived[p, s].astype(F32), 0.0)
                if last:
                    v[b] = ((1.0 - teleport) * total).astype(BF16)
                else:
                    acc[b] = total
                return carry

            lax.fori_loop(0, nb, gather, 0, unroll=4)

    def tail(i, carry):
        part_in, part_out = carry
        at = pl.ds(pl.multiple_of(i * tile, tile), tile)
        ats = pl.ds(i * blocks, blocks)
        grad = (accum[ats] + v[ats].astype(F32)).astype(BF16).reshape(tile, width)
        part_out += nn_dot(act_t[:, at], grad)
        back = nt_dot(grad, w_out[...])
        inner = (back * fac[at, :]).astype(BF16)
        dpre[at, :] = inner
        part_in += nn_dot(feat_t[:, at], inner)
        return part_in, part_out

    part_in, part_out = lax.fori_loop(
        0, rows // tile, tail,
        (jnp.zeros((feats, hid), F32), jnp.zeros((hid, width), F32)))
    low, mid, owners, chunk = owner_layout(n_dom, n_sub, feats + hid)
    split = feats // chunk
    gsend[0:split] = (part_in * norm_scale).reshape(split, chunk, hid).astype(BF16)
    gsend[split:owners] = (part_out * norm_scale).reshape(owners - split, chunk, width).astype(BF16)

    def each_owner(fn):
        for j in range(mid):
            def body(i, carry, j=j):
                d = lax.rem(my_dom + i, n_dom)
                q = d * mid + j
                fit = q < owners if n_dom * mid > owners else None
                other = (i > 0) | (my_sub != low + j)
                pl.when(other if fit is None else other & fit)(lambda: fn(d, low + j, q))
                return carry
            lax.fori_loop(0, n_dom, body, 0)

    my_chunk = my_dom * mid + my_sub - low
    owning = (my_sub >= low) & (my_sub < low + mid)
    if n_dom * mid > owners:
        owning = owning & (my_chunk < owners)

    def part_copy(d, z, q, slot):
        return pltpu.make_async_remote_copy(
            src_ref=gsend.at[q], dst_ref=gparts.at[slot], send_sem=part_send.at[q],
            recv_sem=part_recv.at[slot], device_id=(d, z), device_id_type=MESH)

    def sum_copy(d, z, t, q):
        return pltpu.make_async_remote_copy(
            src_ref=gred, dst_ref=gfull.at[q], send_sem=sum_send.at[t],
            recv_sem=sum_recv.at[q], device_id=(d, z), device_id_type=MESH)

    each_owner(lambda d, z, q: part_copy(d, z, q, me).start())
    dpre_copy = pltpu.make_async_copy(dpre, dpre_hbm, local_sem.at[0])
    dpre_copy.start()

    def wait_sends(d, z, t):
        id_copy(d, z, t, t).wait_send()
        block_copy(0, d, z, t, t).wait_send()
        block_copy(1, d, z, t, t).wait_send()

    each_peer(wait_sends)

    def reduce():
        gparts[me] = gsend[my_chunk]
        each_peer(lambda d, z, s: part_copy(d, z, 0, s).wait_recv())
        total = jnp.sum(gparts[...].astype(F32), axis=0).astype(BF16)
        gred[...] = total
        gfull[my_chunk] = total
        each_peer(lambda d, z, t: sum_copy(d, z, t, my_chunk).start())

    pl.when(owning)(reduce)
    each_owner(lambda d, z, q: part_copy(d, z, q, me).wait_send())
    each_owner(lambda d, z, q: sum_copy(d, z, 0, q).wait_recv())
    pl.when(owning)(lambda: each_peer(lambda d, z, t: sum_copy(d, z, t, my_chunk).wait_send()))
    dpre_copy.wait()


def finish(dpre_ref, w_in_ref, gfull_ref, ig_hbm, gin_hbm, gout_hbm, ig, gin, gout, sems):
    owners, chunk, _ = gfull_ref.shape
    split = gin.shape[0] // chunk
    rows = ig.shape[0]
    pieces = 4 if rows % 64 == 0 else 1
    size = rows // pieces
    gin[...] = gfull_ref[0:split].astype(F32).reshape(gin.shape)
    gout[...] = gfull_ref[split:owners].astype(F32).reshape(gout.shape)
    copies = [pltpu.make_async_copy(gin, gin_hbm, sems.at[0]), pltpu.make_async_copy(gout, gout_hbm, sems.at[1])]
    copies[0].start()
    copies[1].start()
    for i in range(pieces):
        at = pl.ds(i * size, size)
        ig[at, :] = nt_dot(dpre_ref[at, :], w_in_ref[...]).astype(BF16)
        copies.append(pltpu.make_async_copy(ig.at[at, :], ig_hbm.at[at, :], sems.at[2 + i]))
        copies[-1].start()
    for copy in copies:
        copy.wait()


def on_device(n_dom, n_sub, upstream, features, w_in, w_out, inner_adj, cut_tiles, cut_list, cut_count):
    n = n_dom * n_sub
    rows, width = upstream.shape
    entries, blk, _ = cut_tiles.shape
    nb = rows // blk
    feats, hid = w_in.shape
    _, _, owners, chunk = owner_layout(n_dom, n_sub, feats + hid)
    lanes = 128 * -(-n // 128)
    vmem = pl.BlockSpec(memory_space=pltpu.VMEM)
    hbm = pl.BlockSpec(memory_space=pl.ANY)
    scratch = [
        pltpu.VMEM((3, entries), I32),
        pltpu.SMEM((1,), I32),
        pltpu.VMEM((2, lanes), I32),
        pltpu.SMEM((2, lanes), I32),
        pltpu.VMEM(cut_tiles.shape, BF16),
        pltpu.VMEM(w_in.shape, BF16),
        pltpu.VMEM(w_out.shape, BF16),
        pltpu.VMEM(inner_adj.shape, BF16),
        pltpu.VMEM(features.shape, BF16),
        pltpu.VMEM((nb, blk, width), BF16),
        pltpu.VMEM((2, n, blk, width), BF16),
        pltpu.VMEM((2, n, blk, width), BF16),
        pltpu.VMEM((n, 1, 128), I32),
        pltpu.VMEM((n, 1, 128), I32),
        pltpu.VMEM((nb, blk, width), F32),
        pltpu.VMEM((nb, blk, width), F32),
        pltpu.VMEM((rows, hid), F32),
        pltpu.VMEM((hid, rows), BF16),
        pltpu.VMEM((feats, rows), BF16),
        pltpu.VMEM((rows, hid), BF16),
        pltpu.VMEM((owners, chunk, hid), BF16),
        pltpu.VMEM((n, chunk, hid), BF16),
        pltpu.VMEM((chunk, hid), BF16),
        pltpu.SemaphoreType.DMA((8,)),
        pltpu.SemaphoreType.DMA((2, n)),
        pltpu.SemaphoreType.DMA((2, n)),
        pltpu.SemaphoreType.DMA((n,)),
        pltpu.SemaphoreType.DMA((n,)),
        pltpu.SemaphoreType.DMA((owners,)),
        pltpu.SemaphoreType.DMA((n,)),
        pltpu.SemaphoreType.DMA((n,)),
        pltpu.SemaphoreType.DMA((owners,)),
    ]
    dpre, sums = pl.pallas_call(
        functools.partial(kernel, n_dom, n_sub, 1.0 / math.sqrt(rows * n)),
        out_shape=(
            jax.ShapeDtypeStruct((rows, hid), BF16),
            jax.ShapeDtypeStruct((owners, chunk, hid), BF16),
        ),
        in_specs=[hbm] * 8,
        out_specs=(hbm, vmem),
        scratch_shapes=scratch,
        compiler_params=pltpu.CompilerParams(collective_id=0, has_side_effects=True),
    )(cut_list.T, cut_count, upstream.reshape(nb, blk, width), cut_tiles, w_in, w_out, inner_adj, features)
    return pl.pallas_call(
        finish,
        out_shape=(
            jax.ShapeDtypeStruct((rows, feats), BF16),
            jax.ShapeDtypeStruct((feats, hid), F32),
            jax.ShapeDtypeStruct((hid, width), F32),
        ),
        in_specs=[vmem] * 3,
        out_specs=(hbm, hbm, hbm),
        scratch_shapes=[
            pltpu.VMEM((rows, feats), BF16),
            pltpu.VMEM((feats, hid), F32),
            pltpu.VMEM((hid, width), F32),
            pltpu.SemaphoreType.DMA((6,)),
        ],
    )(dpre, w_in, sums)


def solution(mesh):
    both = ("dom", "sub")
    placed = (
        P(both, None),
        P(both, None),
        P(),
        P(),
        P(both, None),
        P(both, None, None),
        P(both, None),
        P(both),
    )
    return jax.shard_map(
        functools.partial(on_device, mesh.shape["dom"], mesh.shape["sub"]),
        mesh=mesh,
        in_specs=placed,
        out_specs=(P(both, None), P(), P()),
        check_vma=False,
    )
```

time: 124 us -> 121 us (0.976)
  other arithmetic: 1.57 us -> 0 us
where the time goes in v1:
time: 121 us
  Pallas kernels  119 us (98%)
  between operations  1.29 us (1%)
    pallas_call x1, Pallas kernels, on_device(): pl.pallas_call(functools.partial(kernel, n_dom, n_sub, 1.0 / math.sqrt(ro...  117 us

profile of v1, /device:TPU:0, one launch (start us, length us, event | category | flops | bytes accessed | tf_op | source)
XLA Modules:
  0.0 120.6 jit_solution(8384889428142629528)
XLA Ops:
  1.3 117.2 %shard_map.103 = (bf16[2048,128]{1,0:T(8,128)(2,1)}, bf16[16,16,128]{2,1,0:T(8,128)(2,1)}) custom-call(s32[3,24]{1,0:T(4,128)} %bitcast.3, s32[1]{0:T(128)S(6)} %copy.11.count_hbm, bf16[16,128,128]{2,1,0:T(8,128)(2,1)} %bitcast.2, bf16[24,128,128]{2,1,0:T(8,128)(2,1)} %tiles_hbm.1, bf16[128,128]{1,0:T(8,128)(2,1)} %w_in_ref.1, bf16[128,128]{1,0:T(8,128)(2,1)} %w_out_hbm.1, ...), custom_call_target="tpu_custom_call" | custom-call | tf_op jit(solution)/shard_map/pallas_call | solution.py:348
  118.5 2.1 %shard_map.104 = (bf16[2048,128]{1,0:T(8,128)(2,1)}, f32[128,128]{1,0:T(8,128)}, f32[128,128]{1,0:T(8,128)}) custom-call(bf16[2048,128]{1,0:T(8,128)(2,1)} %get-tuple-element.5.dpre_ref, bf16[128,128]{1,0:T(8,128)(2,1)} %w_in_ref.1, bf16[16,16,128]{2,1,0:T(8,128)(2,1)} %get-tuple-element.6.gfull_ref), custom_call_target="tpu_custom_call" | custom-call | tf_op jit(solution)/shard_map/pallas_call | solution.py:359

commit v2 on v1

--- a/solution.py
+++ b/solution.py
@@ -31,14 +31,29 @@
     return low, width, grad_rows // chunk, chunk
 
 
+def arrival_groups(n_dom, n_sub):
+    half = n_dom // 2
+    groups = [[(0, 1, n_dom)]] if n_dom > 1 else []
+    for m in reversed(range(3, n_sub)):
+        groups += [[(m, 0, half)], [(m, half, n_dom)]] if half else [[(m, 0, n_dom)]]
+    left = [m for m in (2, 1) if m < n_sub]
+    cuts = sorted({0, half, half + half // 2, n_dom - 1, n_dom})
+    for start, end in zip(cuts[:-1], cuts[1:]):
+        if end == n_dom:
+            groups.append([(m, start, end) for m in left])
+        else:
+            groups += [[(m, start, end)] for m in left]
+    return [group for group in groups if group]
+
+
 def kernel(
     n_dom, n_sub, norm_scale,
     list_hbm, count_hbm, up_hbm, tiles_hbm, w_in_hbm, w_out_hbm, adj_hbm, feat_hbm,
-    dpre_hbm, gfull,
+    ig_hbm, gfull,
     list_v, count_s, idx_v, idx_s, tiles, w_in, w_out,
-    adj, feat, v, outb, arrived, ids_out, ids_in, acc, accum, fac, act_t, feat_t, dpre,
+    adj, feat, v, outb, arrived, ids_out, ids_in, acc, accum, fac, act_t, feat_t, dpre, ig,
     gsend, gparts, gred,
-    local_sem, send_sem, recv_sem, id_send, id_recv, part_send, part_recv, sum_send, sum_recv,
+    local_sem, send_sem, recv_sem, small_sem,
 ):
     n = n_dom * n_sub
     my_dom, my_sub = lax.axis_index("dom"), lax.axis_index("sub")
@@ -51,9 +66,8 @@
     paired = n_sub & (n_sub - 1) == 0
     pairings = list(reversed(range(n_sub)))
     early = pairings[: n_sub // 2] if n_sub > 1 else []
-    arrivals = [(0, 1, n_dom)]
-    for m in pairings[:-1]:
-        arrivals += [(m, i, min(i + 2, n_dom)) for i in range(0, n_dom, 2)] if m == 1 else [(m, 0, n_dom // 2), (m, n_dom // 2, n_dom)]
+    groups = arrival_groups(n_dom, n_sub)
+    group_of = {(m, i): k for k, pieces in enumerate(groups) for m, start, end in pieces for i in range(start, end)}
 
     def partner(m, sign):
         if not paired:
@@ -72,13 +86,20 @@
 
     def each_peer(fn, chosen=None):
         for m in pairings if chosen is None else chosen:
-            def body(i, carry, m=m):
-                fn(*peer(m, i))
-                return carry
-            lax.fori_loop(1 if m == 0 else 0, n_dom, body, 0, unroll=m != 0)
+            i = 1 if m == 0 else 0
+            while i < n_dom:
+                k = group_of[m, i]
+                end = i
+                while end < n_dom and group_of[m, end] == k:
+                    end += 1
+                def body(i, carry, m=m, k=k):
+                    fn(*peer(m, i), k)
+                    return carry
+                lax.fori_loop(i, end, body, 0, unroll=m != 0)
+                i = end
 
     barrier = pltpu.get_barrier_semaphore()
-    each_peer(lambda d, z, t: pl.semaphore_signal(
+    each_peer(lambda d, z, t, k: pl.semaphore_signal(
         barrier, inc=1, device_id=(d, z), device_id_type=MESH))
 
     loads = [
@@ -118,13 +139,18 @@
 
     def id_copy(d, z, t, slot):
         return pltpu.make_async_remote_copy(
-            src_ref=ids_out.at[t], dst_ref=ids_in.at[slot], send_sem=id_send.at[t],
-            recv_sem=id_recv.at[slot], device_id=(d, z), device_id_type=MESH)
-
-    def block_copy(p, d, z, t, slot):
+            src_ref=ids_out.at[t], dst_ref=ids_in.at[slot], send_sem=small_sem.at[0],
+            recv_sem=small_sem.at[1], device_id=(d, z), device_id_type=MESH)
+
+    def block_copy(p, d, z, t, k):
         return pltpu.make_async_remote_copy(
-            src_ref=outb.at[p, t], dst_ref=arrived.at[p, slot], send_sem=send_sem.at[p, t],
-            recv_sem=recv_sem.at[p, slot], device_id=(d, z), device_id_type=MESH)
+            src_ref=outb.at[p, t], dst_ref=arrived.at[p, me], send_sem=send_sem.at[p],
+            recv_sem=recv_sem.at[p, k], device_id=(d, z), device_id_type=MESH)
+
+    def many(ref, count, sem):
+        return pltpu.make_async_remote_copy(
+            src_ref=ref.at[pl.ds(0, count)], dst_ref=ref.at[pl.ds(0, count)], send_sem=sem,
+            recv_sem=sem, device_id=(my_dom, my_sub), device_id_type=MESH)
 
     def multiply(p, t):
         outb[p, t] = nn_dot(tiles[idx_s[1, t]], v[idx_s[0, t]]).astype(BF16)
@@ -132,26 +158,22 @@
     idx_copy.wait()
     up_load.wait()
     tiles_load.wait()
-    each_peer(lambda d, z, t: multiply(0, t), early)
+    each_peer(lambda d, z, t, k: multiply(0, t), early)
     pl.semaphore_wait(barrier, n - 1)
 
-    def send_early(d, z, t):
-        id_copy(d, z, t, me).start()
-        block_copy(0, d, z, t, me).start()
-
-    each_peer(send_early, early)
+    each_peer(lambda d, z, t, k: id_copy(d, z, t, me).start())
+    each_peer(lambda d, z, t, k: block_copy(0, d, z, t, k).start(), early)
     late = [m for m in pairings if m not in early]
 
     for step in range(STEPS):
         p = step % 2
 
-        def send(d, z, t):
-            if step >= 2:
-                block_copy(p, d, z, t, t).wait_send()
-            if step == 0:
-                id_copy(d, z, t, me).start()
+        def send(d, z, t, k):
             multiply(p, t)
-            block_copy(p, d, z, t, me).start()
+            block_copy(p, d, z, t, k).start()
+
+        if step >= 2:
+            many(outb.at[p], n - 1, send_sem.at[p]).wait_send()
 
         each_peer(send, late if step == 0 else pairings)
 
@@ -183,24 +205,20 @@
 
         lax.fori_loop(0, rows // tile, local, 0)
 
-        for m, start, end in arrivals:
-            last = (m, start, end) == arrivals[-1]
-
-            def arrive(i, carry):
-                d, z, s = peer(m, i, -1)
-                if step == 0:
-                    id_copy(d, z, s, s).wait_recv()
-                block_copy(p, d, z, s, s).wait_recv()
-                return carry
-
-            lax.fori_loop(start, end, arrive, 0)
+        for k, pieces in enumerate(groups):
+            last = k == len(groups) - 1
+            if step == 0 and k == 0:
+                many(ids_in, n - 1, small_sem.at[1]).wait_recv()
+            count = sum(end - start for _, start, end in pieces)
+            many(arrived.at[p], count, recv_sem.at[p, k]).wait_recv()
 
             def gather(b, carry):
                 total = acc[b]
-                for i in range(start, end):
-                    s = peer(m, i, -1)[2]
-                    match = ids_in[s, 0:1, :] == b
-                    total += jnp.where(match, arrived[p, s].astype(F32), 0.0)
+                for m, start, end in pieces:
+                    for i in range(start, end):
+                        s = peer(m, i, -1)[2]
+                        match = ids_in[s, 0:1, :] == b
+                        total += jnp.where(match, arrived[p, s].astype(F32), 0.0)
                 if last:
                     v[b] = ((1.0 - teleport) * total).astype(BF16)
                 else:
@@ -223,7 +241,7 @@
 
     part_in, part_out = lax.fori_loop(
         0, rows // tile, tail,
-        (jnp.zeros((feats, hid), F32), jnp.zeros((hid, width), F32)))
+        (jnp.zeros((feats, hid), F32), jnp.zeros((hid, width), F32)), unroll=True)
     low, mid, owners, chunk = owner_layout(n_dom, n_sub, feats + hid)
     split = feats // chunk
     gsend[0:split] = (part_in * norm_scale).reshape(split, chunk, hid).astype(BF16)
@@ -247,58 +265,73 @@
 
     def part_copy(d, z, q, slot):
         return pltpu.make_async_remote_copy(
-            src_ref=gsend.at[q], dst_ref=gparts.at[slot], send_sem=part_send.at[q],
-            recv_sem=part_recv.at[slot], device_id=(d, z), device_id_type=MESH)
-
-    def sum_copy(d, z, t, q):
+            src_ref=gsend.at[q], dst_ref=gparts.at[slot], send_sem=small_sem.at[2],
+            recv_sem=small_sem.at[3], device_id=(d, z), device_id_type=MESH)
+
+    def sum_copy(d, z, q):
         return pltpu.make_async_remote_copy(
-            src_ref=gred, dst_ref=gfull.at[q], send_sem=sum_send.at[t],
-            recv_sem=sum_recv.at[q], device_id=(d, z), device_id_type=MESH)
+            src_ref=gred, dst_ref=gfull.at[q], send_sem=small_sem.at[4],
+            recv_sem=small_sem.at[5], device_id=(d, z), device_id_type=MESH)
 
     each_owner(lambda d, z, q: part_copy(d, z, q, me).start())
-    dpre_copy = pltpu.make_async_copy(dpre, dpre_hbm, local_sem.at[0])
-    dpre_copy.start()
-
-    def wait_sends(d, z, t):
-        id_copy(d, z, t, t).wait_send()
-        block_copy(0, d, z, t, t).wait_send()
-        block_copy(1, d, z, t, t).wait_send()
-
-    each_peer(wait_sends)
+
+    def project(i, carry):
+        at = pl.ds(pl.multiple_of(i * tile, tile), tile)
+        ig[at, :] = nt_dot(dpre[at, :], w_in[...]).astype(BF16)
+        return carry
+
+    lax.fori_loop(0, rows // tile, project, 0)
+    ig_copy = pltpu.make_async_copy(ig, ig_hbm, local_sem.at[0])
+    ig_copy.start()
+    many(ids_out, n - 1, small_sem.at[0]).wait_send()
+    many(outb.at[0], n - 1, send_sem.at[0]).wait_send()
+    many(outb.at[1], n - 1, send_sem.at[1]).wait_send()
 
     def reduce():
         gparts[me] = gsend[my_chunk]
-        each_peer(lambda d, z, s: part_copy(d, z, 0, s).wait_recv())
+        many(gparts, n - 1, small_sem.at[3]).wait_recv()
         total = jnp.sum(gparts[...].astype(F32), axis=0).astype(BF16)
         gred[...] = total
         gfull[my_chunk] = total
-        each_peer(lambda d, z, t: sum_copy(d, z, t, my_chunk).start())
+        each_peer(lambda d, z, t, k: sum_copy(d, z, my_chunk).start())
+        many(gsend, owners - 1, small_sem.at[2]).wait_send()
+        many(gfull, owners - 1, small_sem.at[5]).wait_recv()
+        many(gparts, n - 1, small_sem.at[4]).wait_send()
+
+    def follow():
+        many(gsend, owners, small_sem.at[2]).wait_send()
+        many(gfull, owners, small_sem.at[5]).wait_recv()
 
     pl.when(owning)(reduce)
-    each_owner(lambda d, z, q: part_copy(d, z, q, me).wait_send())
-    each_owner(lambda d, z, q: sum_copy(d, z, 0, q).wait_recv())
-    pl.when(owning)(lambda: each_peer(lambda d, z, t: sum_copy(d, z, t, my_chunk).wait_send()))
-    dpre_copy.wait()
-
-
-def finish(dpre_ref, w_in_ref, gfull_ref, ig_hbm, gin_hbm, gout_hbm, ig, gin, gout, sems):
-    owners, chunk, _ = gfull_ref.shape
+    pl.when(jnp.logical_not(owning))(follow)
+    ig_copy.wait()
+
+
+PIECES = 4
+
+
+def finish(ig_in, sums_in, ig_out, gin_out, gout_out, ig, sums, gin, gout, sems):
+    owners, chunk, _ = sums.shape
     split = gin.shape[0] // chunk
-    rows = ig.shape[0]
-    pieces = 4 if rows % 64 == 0 else 1
-    size = rows // pieces
-    gin[...] = gfull_ref[0:split].astype(F32).reshape(gin.shape)
-    gout[...] = gfull_ref[split:owners].astype(F32).reshape(gout.shape)
-    copies = [pltpu.make_async_copy(gin, gin_hbm, sems.at[0]), pltpu.make_async_copy(gout, gout_hbm, sems.at[1])]
-    copies[0].start()
-    copies[1].start()
-    for i in range(pieces):
-        at = pl.ds(i * size, size)
-        ig[at, :] = nt_dot(dpre_ref[at, :], w_in_ref[...]).astype(BF16)
-        copies.append(pltpu.make_async_copy(ig.at[at, :], ig_hbm.at[at, :], sems.at[2 + i]))
-        copies[-1].start()
-    for copy in copies:
-        copy.wait()
+    size = ig.shape[0] // PIECES
+    pieces = [pl.ds(i * size, size) for i in range(PIECES)]
+    sums_load = pltpu.make_async_copy(sums_in, sums, sems.at[0])
+    loads = [pltpu.make_async_copy(ig_in.at[at, :], ig.at[at, :], sems.at[3 + i]) for i, at in enumerate(pieces)]
+    stores = [pltpu.make_async_copy(ig.at[at, :], ig_out.at[at, :], sems.at[3 + i]) for i, at in enumerate(pieces)]
+    stores += [pltpu.make_async_copy(gin, gin_out, sems.at[1]), pltpu.make_async_copy(gout, gout_out, sems.at[2])]
+    sums_load.start()
+    for load in loads:
+        load.start()
+    sums_load.wait()
+    gin[...] = sums[0:split].astype(F32).reshape(gin.shape)
+    stores[-2].start()
+    gout[...] = sums[split:owners].astype(F32).reshape(gout.shape)
+    stores[-1].start()
+    for load, store in zip(loads, stores):
+        load.wait()
+        store.start()
+    for store in stores:
+        store.wait()
 
 
 def on_device(n_dom, n_sub, upstream, features, w_in, w_out, inner_adj, cut_tiles, cut_list, cut_count):
@@ -332,23 +365,19 @@
         pltpu.VMEM((hid, rows), BF16),
         pltpu.VMEM((feats, rows), BF16),
         pltpu.VMEM((rows, hid), BF16),
+        pltpu.VMEM((rows, feats), BF16),
         pltpu.VMEM((owners, chunk, hid), BF16),
         pltpu.VMEM((n, chunk, hid), BF16),
         pltpu.VMEM((chunk, hid), BF16),
         pltpu.SemaphoreType.DMA((8,)),
-        pltpu.SemaphoreType.DMA((2, n)),
-        pltpu.SemaphoreType.DMA((2, n)),
-        pltpu.SemaphoreType.DMA((n,)),
-        pltpu.SemaphoreType.DMA((n,)),
-        pltpu.SemaphoreType.DMA((owners,)),
-        pltpu.SemaphoreType.DMA((n,)),
-        pltpu.SemaphoreType.DMA((n,)),
-        pltpu.SemaphoreType.DMA((owners,)),
+        pltpu.SemaphoreType.DMA((2,)),
+        pltpu.SemaphoreType.DMA((2, len(arrival_groups(n_dom, n_sub)))),
+        pltpu.SemaphoreType.DMA((6,)),
     ]
-    dpre, sums = pl.pallas_call(
+    ig, sums = pl.pallas_call(
         functools.partial(kernel, n_dom, n_sub, 1.0 / math.sqrt(rows * n)),
         out_shape=(
-            jax.ShapeDtypeStruct((rows, hid), BF16),
+            jax.ShapeDtypeStruct((rows, feats), BF16),
             jax.ShapeDtypeStruct((owners, chunk, hid), BF16),
         ),
         in_specs=[hbm] * 8,
@@ -363,15 +392,16 @@
             jax.ShapeDtypeStruct((feats, hid), F32),
             jax.ShapeDtypeStruct((hid, width), F32),
         ),
-        in_specs=[vmem] * 3,
+        in_specs=[hbm, hbm],
         out_specs=(hbm, hbm, hbm),
         scratch_shapes=[
             pltpu.VMEM((rows, feats), BF16),
+            pltpu.VMEM(sums.shape, BF16),
             pltpu.VMEM((feats, hid), F32),
             pltpu.VMEM((hid, width), F32),
-            pltpu.SemaphoreType.DMA((6,)),
+            pltpu.SemaphoreType.DMA((3 + PIECES,)),
         ],
-    )(dpre, w_in, sums)
+    )(ig, sums)
 
 
 def solution(mesh):

time: 121 us -> 115 us (0.950)
  Pallas kernels: 119 us -> 114 us
    pallas_call x1, Pallas kernels: 117 us -> 112 us  [on_device(): pl.pallas_call(functools.partial(kernel, n_dom, n_sub, 1.0 / math.sqrt(ro...]
where the time goes in v2:
time: 115 us
  Pallas kernels  114 us (99%)
  between operations  1.29 us (1%)
    pallas_call x1, Pallas kernels, on_device(): pl.pallas_call(functools.partial(kernel, n_dom, n_sub, 1.0 / math.sqrt(ro...  112 us

profile of v2, /device:TPU:0, one launch (start us, length us, event | category | flops | bytes accessed | tf_op | source)
XLA Modules:
  0.0 114.8 jit_solution(17017547752415215536)
XLA Ops:
  1.3 111.7 %shard_map.103 = (bf16[2048,128]{1,0:T(8,128)(2,1)}, bf16[16,16,128]{2,1,0:T(8,128)(2,1)}) custom-call(s32[3,24]{1,0:T(4,128)} %bitcast.3, s32[1]{0:T(128)S(6)} %copy.11.count_hbm, bf16[16,128,128]{2,1,0:T(8,128)(2,1)} %bitcast.2, bf16[24,128,128]{2,1,0:T(8,128)(2,1)} %tiles_hbm.1, bf16[128,128]{1,0:T(8,128)(2,1)} %w_in_hbm.1, bf16[128,128]{1,0:T(8,128)(2,1)} %w_out_hbm.1, ...), custom_call_target="tpu_custom_call" | custom-call | tf_op jit(solution)/shard_map/pallas_call | solution.py:377
  113.0 1.9 %shard_map.104 = (bf16[2048,128]{1,0:T(8,128)(2,1)}, f32[128,128]{1,0:T(8,128)}, f32[128,128]{1,0:T(8,128)}) custom-call(bf16[2048,128]{1,0:T(8,128)(2,1)} %get-tuple-element.5.ig_in, bf16[16,16,128]{2,1,0:T(8,128)(2,1)} %get-tuple-element.6.sums_in), custom_call_target="tpu_custom_call" | custom-call | tf_op jit(solution)/shard_map/pallas_call | solution.py:388

commit v3 on v2

--- a/solution.py
+++ b/solution.py
@@ -212,49 +212,43 @@
             count = sum(end - start for _, start, end in pieces)
             many(arrived.at[p], count, recv_sem.at[p, k]).wait_recv()
 
-            def gather(b, carry):
+            def summed(b):
                 total = acc[b]
                 for m, start, end in pieces:
                     for i in range(start, end):
                         s = peer(m, i, -1)[2]
                         match = ids_in[s, 0:1, :] == b
                         total += jnp.where(match, arrived[p, s].astype(F32), 0.0)
+                return total
+
+            def gather(b, carry):
                 if last:
-                    v[b] = ((1.0 - teleport) * total).astype(BF16)
+                    v[b] = ((1.0 - teleport) * summed(b)).astype(BF16)
                 else:
-                    acc[b] = total
+                    acc[b] = summed(b)
                 return carry
 
-            lax.fori_loop(0, nb, gather, 0, unroll=4)
-
-    def tail(i, carry):
-        part_in, part_out = carry
-        at = pl.ds(pl.multiple_of(i * tile, tile), tile)
-        ats = pl.ds(i * blocks, blocks)
-        grad = (accum[ats] + v[ats].astype(F32)).astype(BF16).reshape(tile, width)
-        part_out += nn_dot(act_t[:, at], grad)
-        back = nt_dot(grad, w_out[...])
-        inner = (back * fac[at, :]).astype(BF16)
-        dpre[at, :] = inner
-        part_in += nn_dot(feat_t[:, at], inner)
-        return part_in, part_out
-
-    part_in, part_out = lax.fori_loop(
-        0, rows // tile, tail,
-        (jnp.zeros((feats, hid), F32), jnp.zeros((hid, width), F32)), unroll=True)
+            if not (last and step == STEPS - 1):
+                lax.fori_loop(0, nb, gather, 0, unroll=4)
+
+    def head_grad(b):
+        final = ((1.0 - teleport) * summed(b)).astype(BF16)
+        return (accum[b] + final.astype(F32)).astype(BF16)
+
     low, mid, owners, chunk = owner_layout(n_dom, n_sub, feats + hid)
     split = feats // chunk
-    gsend[0:split] = (part_in * norm_scale).reshape(split, chunk, hid).astype(BF16)
-    gsend[split:owners] = (part_out * norm_scale).reshape(owners - split, chunk, width).astype(BF16)
-
-    def each_owner(fn):
-        for j in range(mid):
+
+    def each_owner(fn, wanted=None):
+        for k in range(mid):
+            j = jnp.where(my_sub < low + (mid + 1) // 2, mid - 1 - k, k)
+
             def body(i, carry, j=j):
                 d = lax.rem(my_dom + i, n_dom)
                 q = d * mid + j
                 fit = q < owners if n_dom * mid > owners else None
                 other = (i > 0) | (my_sub != low + j)
-                pl.when(other if fit is None else other & fit)(lambda: fn(d, low + j, q))
+                other = other if fit is None else other & fit
+                pl.when(other if wanted is None else other & wanted(q))(lambda: fn(d, low + j, q))
                 return carry
             lax.fori_loop(0, n_dom, body, 0)
 
@@ -273,7 +267,28 @@
             src_ref=gred, dst_ref=gfull.at[q], send_sem=small_sem.at[4],
             recv_sem=small_sem.at[5], device_id=(d, z), device_id_type=MESH)
 
-    each_owner(lambda d, z, q: part_copy(d, z, q, me).start())
+    def tail_out(i, part_out):
+        at = pl.ds(pl.multiple_of(i * tile, tile), tile)
+        ats = pl.ds(i * blocks, blocks)
+        grad = jnp.concatenate([head_grad(i * blocks + j) for j in range(blocks)], axis=0)
+        v[ats] = grad.reshape(blocks, blk, width)
+        return part_out + nn_dot(act_t[:, at], grad)
+
+    part_out = lax.fori_loop(0, rows // tile, tail_out, jnp.zeros((hid, width), F32), unroll=True)
+    gsend[split:owners] = (part_out * norm_scale).reshape(owners - split, chunk, width).astype(BF16)
+    each_owner(lambda d, z, q: part_copy(d, z, q, me).start(), lambda q: q >= split)
+
+    def tail_in(i, part_in):
+        at = pl.ds(pl.multiple_of(i * tile, tile), tile)
+        ats = pl.ds(i * blocks, blocks)
+        back = nt_dot(v[ats].reshape(tile, width), w_out[...])
+        inner = (back * fac[at, :]).astype(BF16)
+        dpre[at, :] = inner
+        return part_in + nn_dot(feat_t[:, at], inner)
+
+    part_in = lax.fori_loop(0, rows // tile, tail_in, jnp.zeros((feats, hid), F32), unroll=True)
+    gsend[0:split] = (part_in * norm_scale).reshape(split, chunk, hid).astype(BF16)
+    each_owner(lambda d, z, q: part_copy(d, z, q, me).start(), lambda q: q < split)
 
     def project(i, carry):
         at = pl.ds(pl.multiple_of(i * tile, tile), tile)
@@ -292,11 +307,13 @@
         many(gparts, n - 1, small_sem.at[3]).wait_recv()
         total = jnp.sum(gparts[...].astype(F32), axis=0).astype(BF16)
         gred[...] = total
-        gfull[my_chunk] = total
+        mine = pltpu.make_async_copy(gred, gfull.at[my_chunk], local_sem.at[1])
+        mine.start()
         each_peer(lambda d, z, t, k: sum_copy(d, z, my_chunk).start())
         many(gsend, owners - 1, small_sem.at[2]).wait_send()
         many(gfull, owners - 1, small_sem.at[5]).wait_recv()
         many(gparts, n - 1, small_sem.at[4]).wait_send()
+        mine.wait()
 
     def follow():
         many(gsend, owners, small_sem.at[2]).wait_send()
@@ -307,7 +324,7 @@
     ig_copy.wait()
 
 
-PIECES = 4
+PIECES = 8
 
 
 def finish(ig_in, sums_in, ig_out, gin_out, gout_out, ig, sums, gin, gout, sems):
@@ -381,7 +398,7 @@
             jax.ShapeDtypeStruct((owners, chunk, hid), BF16),
         ),
         in_specs=[hbm] * 8,
-        out_specs=(hbm, vmem),
+        out_specs=(hbm, hbm),
         scratch_shapes=scratch,
         compiler_params=pltpu.CompilerParams(collective_id=0, has_side_effects=True),
     )(cut_list.T, cut_count, upstream.reshape(nb, blk, width), cut_tiles, w_in, w_out, inner_adj, features)

time: 115 us -> 114 us (level)
  Pallas kernels: 114 us -> 112 us
    pallas_call x1, Pallas kernels: 112 us -> 110 us  [on_device(): pl.pallas_call(functools.partial(kernel, n_dom, n_sub, 1.0 / math.sqrt(ro...]
where the time goes in v3:
time: 114 us
  Pallas kernels  112 us (98%)
  between operations  1.29 us (1%)
    pallas_call x1, Pallas kernels, on_device(): pl.pallas_call(functools.partial(kernel, n_dom, n_sub, 1.0 / math.sqrt(ro...  110 us

profile of v3, /device:TPU:0, one launch (start us, length us, event | category | flops | bytes accessed | tf_op | source)
XLA Modules:
  0.0 113.6 jit_solution(442430289414883688)
XLA Ops:
  1.3 110.5 %shard_map.103 = (bf16[2048,128]{1,0:T(8,128)(2,1)}, bf16[16,16,128]{2,1,0:T(8,128)(2,1)}) custom-call(s32[3,24]{1,0:T(4,128)} %bitcast.3, s32[1]{0:T(128)S(6)} %copy.11.count_hbm, bf16[16,128,128]{2,1,0:T(8,128)(2,1)} %bitcast.2, bf16[24,128,128]{2,1,0:T(8,128)(2,1)} %tiles_hbm.1, bf16[128,128]{1,0:T(8,128)(2,1)} %w_in_hbm.1, bf16[128,128]{1,0:T(8,128)(2,1)} %w_out_hbm.1, ...), custom_call_target="tpu_custom_call" | custom-call | tf_op jit(solution)/shard_map/pallas_call | solution.py:394
  111.7 1.8 %shard_map.104 = (bf16[2048,128]{1,0:T(8,128)(2,1)}, f32[128,128]{1,0:T(8,128)}, f32[128,128]{1,0:T(8,128)}) custom-call(bf16[2048,128]{1,0:T(8,128)(2,1)} %get-tuple-element.5.ig_in, bf16[16,16,128]{2,1,0:T(8,128)(2,1)} %get-tuple-element.6.sums_in), custom_call_target="tpu_custom_call" | custom-call | tf_op jit(solution)/shard_map/pallas_call | solution.py:405

commit v4 on v3

--- a/solution.py
+++ b/solution.py
@@ -37,12 +37,9 @@
     for m in reversed(range(3, n_sub)):
         groups += [[(m, 0, half)], [(m, half, n_dom)]] if half else [[(m, 0, n_dom)]]
     left = [m for m in (2, 1) if m < n_sub]
-    cuts = sorted({0, half, half + half // 2, n_dom - 1, n_dom})
+    cuts = sorted({0, half // 2, half, half + half // 2, n_dom - 1, n_dom})
     for start, end in zip(cuts[:-1], cuts[1:]):
-        if end == n_dom:
-            groups.append([(m, start, end) for m in left])
-        else:
-            groups += [[(m, start, end)] for m in left]
+        groups.append([(m, start, end) for m in left])
     return [group for group in groups if group]
 
 
@@ -65,7 +62,7 @@
     blocks = tile // blk
     paired = n_sub & (n_sub - 1) == 0
     pairings = list(reversed(range(n_sub)))
-    early = pairings[: n_sub // 2] if n_sub > 1 else []
+    early = pairings[:-1]
     groups = arrival_groups(n_dom, n_sub)
     group_of = {(m, i): k for k, pieces in enumerate(groups) for m, start, end in pieces for i in range(start, end)}
 
@@ -250,7 +247,7 @@
                 other = other if fit is None else other & fit
                 pl.when(other if wanted is None else other & wanted(q))(lambda: fn(d, low + j, q))
                 return carry
-            lax.fori_loop(0, n_dom, body, 0)
+            lax.fori_loop(0, n_dom, body, 0, unroll=True)
 
     my_chunk = my_dom * mid + my_sub - low
     owning = (my_sub >= low) & (my_sub < low + mid)

time: 114 us -> 113 us (level)
  no operation moved by 1% of the time
where the time goes in v4:
time: 113 us
  Pallas kernels  112 us (99%)
  between operations  1.29 us (1%)
    pallas_call x1, Pallas kernels, on_device(): pl.pallas_call(functools.partial(kernel, n_dom, n_sub, 1.0 / math.sqrt(ro...  110 us

profile of v4, /device:TPU:0, one launch (start us, length us, event | category | flops | bytes accessed | tf_op | source)
XLA Modules:
  0.0 113.3 jit_solution(13514174009431376007)
XLA Ops:
  1.3 110.2 %shard_map.103 = (bf16[2048,128]{1,0:T(8,128)(2,1)}, bf16[16,16,128]{2,1,0:T(8,128)(2,1)}) custom-call(s32[3,24]{1,0:T(4,128)} %bitcast.3, s32[1]{0:T(128)S(6)} %copy.11.count_hbm, bf16[16,128,128]{2,1,0:T(8,128)(2,1)} %bitcast.2, bf16[24,128,128]{2,1,0:T(8,128)(2,1)} %tiles_hbm.1, bf16[128,128]{1,0:T(8,128)(2,1)} %w_in_hbm.1, bf16[128,128]{1,0:T(8,128)(2,1)} %w_out_hbm.1, ...), custom_call_target="tpu_custom_call" | custom-call | tf_op jit(solution)/shard_map/pallas_call | solution.py:391
  111.5 1.8 %shard_map.104 = (bf16[2048,128]{1,0:T(8,128)(2,1)}, f32[128,128]{1,0:T(8,128)}, f32[128,128]{1,0:T(8,128)}) custom-call(bf16[2048,128]{1,0:T(8,128)(2,1)} %get-tuple-element.5.ig_in, bf16[16,16,128]{2,1,0:T(8,128)(2,1)} %get-tuple-element.6.sums_in), custom_call_target="tpu_custom_call" | custom-call | tf_op jit(solution)/shard_map/pallas_call | solution.py:402

commit v5 on v3

--- a/solution.py
+++ b/solution.py
@@ -14,10 +14,6 @@
 F32 = jnp.float32
 BF16 = jnp.bfloat16
 I32 = jnp.int32
-
-
-def nt_dot(a, b):
-    return lax.dot_general(a, b, (((1,), (1,)), ((), ())), preferred_element_type=F32)
 
 
 def nn_dot(a, b):
@@ -50,7 +46,7 @@
     n_dom, n_sub, norm_scale,
     list_hbm, count_hbm, up_hbm, tiles_hbm, w_in_hbm, w_out_hbm, adj_hbm, feat_hbm,
     ig_hbm, gfull,
-    list_v, count_s, idx_v, idx_s, tiles, w_in, w_out,
+    list_v, count_s, idx_v, idx_s, tiles, w_in, w_out, w_in_t, w_out_t,
     adj, feat, v, outb, arrived, ids_out, ids_in, acc, accum, fac, act_t, feat_t, dpre, ig,
     gsend, gparts, gred,
     local_sem, send_sem, recv_sem, small_sem,
@@ -181,6 +177,8 @@
             feat_load.wait()
             w_in_load.wait()
             w_out_load.wait()
+            w_out_t[...] = w_out[...].T
+            w_in_t[...] = w_in[...].T
 
             def head(i, carry):
                 at = pl.ds(pl.multiple_of(i * tile, tile), tile)
@@ -281,7 +279,7 @@
     def tail_in(i, part_in):
         at = pl.ds(pl.multiple_of(i * tile, tile), tile)
         ats = pl.ds(i * blocks, blocks)
-        back = nt_dot(v[ats].reshape(tile, width), w_out[...])
+        back = nn_dot(v[ats].reshape(tile, width), w_out_t[...])
         inner = (back * fac[at, :]).astype(BF16)
         dpre[at, :] = inner
         return part_in + nn_dot(feat_t[:, at], inner)
@@ -292,7 +290,7 @@
 
     def project(i, carry):
         at = pl.ds(pl.multiple_of(i * tile, tile), tile)
-        ig[at, :] = nt_dot(dpre[at, :], w_in[...]).astype(BF16)
+        ig[at, :] = nn_dot(dpre[at, :], w_in_t[...]).astype(BF16)
         return carry
 
     lax.fori_loop(0, rows // tile, project, 0)
@@ -369,6 +367,8 @@
         pltpu.VMEM(cut_tiles.shape, BF16),
         pltpu.VMEM(w_in.shape, BF16),
         pltpu.VMEM(w_out.shape, BF16),
+        pltpu.VMEM(w_in.shape[::-1], BF16),
+        pltpu.VMEM(w_out.shape[::-1], BF16),
         pltpu.VMEM(inner_adj.shape, BF16),
         pltpu.VMEM(features.shape, BF16),
         pltpu.VMEM((nb, blk, width), BF16),

time: 114 us -> 114 us (level)
  no operation moved by 1% of the time
where the time goes in v5:
time: 114 us
  Pallas kernels  112 us (98%)
  between operations  1.29 us (1%)
    pallas_call x1, Pallas kernels, on_device(): pl.pallas_call(functools.partial(kernel, n_dom, n_sub, 1.0 / math.sqrt(ro...  110 us

profile of v5, /device:TPU:0, one launch (start us, length us, event | category | flops | bytes accessed | tf_op | source)
XLA Modules:
  0.0 113.5 jit_solution(6745575104517877485)
XLA Ops:
  1.3 110.4 %shard_map.103 = (bf16[2048,128]{1,0:T(8,128)(2,1)}, bf16[16,16,128]{2,1,0:T(8,128)(2,1)}) custom-call(s32[3,24]{1,0:T(4,128)} %bitcast.3, s32[1]{0:T(128)S(6)} %copy.11.count_hbm, bf16[16,128,128]{2,1,0:T(8,128)(2,1)} %bitcast.2, bf16[24,128,128]{2,1,0:T(8,128)(2,1)} %tiles_hbm.1, bf16[128,128]{1,0:T(8,128)(2,1)} %w_in_hbm.1, bf16[128,128]{1,0:T(8,128)(2,1)} %w_out_hbm.1, ...), custom_call_target="tpu_custom_call" | custom-call | tf_op jit(solution)/shard_map/pallas_call | solution.py:394
  111.7 1.8 %shard_map.104 = (bf16[2048,128]{1,0:T(8,128)(2,1)}, f32[128,128]{1,0:T(8,128)}, f32[128,128]{1,0:T(8,128)}) custom-call(bf16[2048,128]{1,0:T(8,128)(2,1)} %get-tuple-element.5.ig_in, bf16[16,16,128]{2,1,0:T(8,128)(2,1)} %get-tuple-element.6.sums_in), custom_call_target="tpu_custom_call" | custom-call | tf_op jit(solution)/shard_map/pallas_call | solution.py:405
